TPU v7x, 512 devices: a whole 4x8x8 slice. The times are simulated.
512 devices in a mesh: crate: 32 (over z, x), board: 16 (over y, core).
Axes of the slice: x: 4, y: 8, z: 8, core: 2. Of those that a mesh axis runs over, the one named last changes fastest.
Arguments:
- voltages: bfloat16 [2048, 65536], P(('crate', 'board')), may hold values from -6 to 6
- wiring: int32 [2048], replicated, may hold values from 0 to 2047, each once
- positions: float32 [2, 2048], replicated, may hold values from -4 to 4
- directions: float32 [2, 512], replicated, may hold values from -1 to 1
- gains: float32 [2, 256, 2048], P(None, 'crate'), may hold values from -6 to 6
- delays: int32 [256, 512], replicated, may hold values from 0 to 31
Outputs:
- dedispersed: float32 [512, 512, 32], P('crate', 'board')
Inputs may be any that keep to these rules, and one draw needn't show every extreme that they name: `wiring`: each of the 2048 antennas is wired to exactly one input row.
All inputs are finite; a program needn't handle non-finite values.
Results may differ from a plain program's by a relative error of at most 0.0096.
Values may be sent and summed in bfloat16 or wider, within the bound.
A program may use at most 64 MiB of HBM per device.

v0:
```python
import math
import jax
import jax.numpy as jnp
from jax import lax
from jax.sharding import PartitionSpec as P

ANTENNA_INPUTS = 2048
FREQ_CHANNELS = 256
FRAME_SAMPLES = 512
BEAMS = 512
DMS = 512
SPECTRUM_BATCHES = 2
BATCH_SPECTRA = 64
AVG = 4
BINS = 16
TB = 32
two_pi = 2.0 * math.pi


def filter_table():
    sample_ids = jnp.arange(FRAME_SAMPLES, dtype=jnp.int32)
    column_ids = jnp.arange(FREQ_CHANNELS, dtype=jnp.int32)
    window = 0.5 - 0.5 * jnp.cos(two_pi / FRAME_SAMPLES * sample_ids.astype(jnp.float32))
    turn_ids = sample_ids[:, None] * column_ids[None, :] % FRAME_SAMPLES
    phase_angle = two_pi / FRAME_SAMPLES * turn_ids.astype(jnp.float32)
    scale_norm_factor = 1.0 / math.sqrt(3.0 * FRAME_SAMPLES / 8.0)
    real_part = window[:, None] * jnp.cos(phase_angle) * scale_norm_factor
    imag_part = -window[:, None] * jnp.sin(phase_angle) * scale_norm_factor
    return jnp.concatenate([real_part, imag_part], axis=1).astype(jnp.bfloat16)


def beam_weights(channel, directions, place_x, place_y, gain_re, gain_im):
    geo_delay = (
        directions[0][:, None] * place_x[None, :] + directions[1][:, None] * place_y[None, :]
    )
    factor = two_pi * (1.0 + channel.astype(jnp.float32) / FREQ_CHANNELS)
    phase_angle = factor * geo_delay
    cosine = jnp.cos(phase_angle)
    sine_value = jnp.sin(phase_angle)
    scale_norm_factor = 1.0 / math.sqrt(ANTENNA_INPUTS)
    weight_re = (
        (gain_re[None, :] * cosine + gain_im[None, :] * sine_value) * scale_norm_factor
    ).astype(jnp.bfloat16)
    weight_im = (
        (gain_im[None, :] * cosine - gain_re[None, :] * sine_value) * scale_norm_factor
    ).astype(jnp.bfloat16)
    return (weight_re, weight_im)


def dedisperse(series, delay_table):
    bin_count = series.shape[2]
    bin_ids = jnp.arange(bin_count, dtype=jnp.int32)
    turn_ids = bin_ids[:, None] * bin_ids[None, :] % bin_count
    phase_angle = two_pi / bin_count * turn_ids.astype(jnp.float32)
    cos_table = jnp.cos(phase_angle)
    sin_table = jnp.sin(phase_angle)
    spec_re = jnp.einsum("bct,tk->kcb", series, cos_table, precision=lax.Precision.HIGHEST)
    spec_im = -jnp.einsum("bct,tk->kcb", series, sin_table, precision=lax.Precision.HIGHEST)

    def per_freq(inputs):
        freq_id, part_re, part_im = inputs
        shift_angle = two_pi / bin_count * (freq_id * delay_table % bin_count).astype(jnp.float32)
        shift_re = jnp.cos(shift_angle)
        shift_im = jnp.sin(shift_angle)
        out_re = jnp.einsum(
            "cd,cb->db", shift_re, part_re, precision=lax.Precision.HIGHEST
        ) - jnp.einsum("cd,cb->db", shift_im, part_im, precision=lax.Precision.HIGHEST)
        out_im = jnp.einsum(
            "cd,cb->db", shift_re, part_im, precision=lax.Precision.HIGHEST
        ) + jnp.einsum("cd,cb->db", shift_im, part_re, precision=lax.Precision.HIGHEST)
        return (out_re, out_im)

    freq_re, freq_im = lax.map(per_freq, (bin_ids, spec_re, spec_im))
    keep_mask = (bin_ids > 0).astype(jnp.float32)[:, None]
    scale_norm_factor = 1.0 / (bin_count * math.sqrt(FREQ_CHANNELS))
    first_term = jnp.einsum(
        "kdb,kt->bdt", freq_re, cos_table * keep_mask, precision=lax.Precision.HIGHEST
    )
    second_term = jnp.einsum(
        "kdb,kt->bdt", freq_im, sin_table * keep_mask, precision=lax.Precision.HIGHEST
    )
    return (first_term - second_term) * scale_norm_factor


def shards(voltages, wiring, positions, directions, gains, delays):
    crate_list = lax.axis_size("crate")
    board_list = lax.axis_size("board")
    crate_index = lax.axis_index("crate")
    board_index = lax.axis_index("board")
    local_antenna = voltages.shape[0]
    channel_groups = SPECTRUM_BATCHES * FREQ_CHANNELS // (crate_list * board_list)
    dft_table = filter_table()
    sample_frames = voltages.reshape(
        local_antenna * SPECTRUM_BATCHES * BATCH_SPECTRA, FRAME_SAMPLES
    )
    spectrum_rows = jnp.dot(sample_frames, dft_table, preferred_element_type=jnp.float32).astype(
        jnp.bfloat16
    )
    spectrum_rows = spectrum_rows.reshape(
        local_antenna, SPECTRUM_BATCHES, BATCH_SPECTRA, 2, FREQ_CHANNELS
    ).transpose(4, 1, 0, 3, 2)
    spectrum_rows = spectrum_rows.reshape(
        crate_list, board_list, channel_groups, local_antenna, 2 * BATCH_SPECTRA
    )
    position_grid = jnp.arange(ANTENNA_INPUTS, dtype=jnp.int32).reshape(
        crate_list, board_list, local_antenna
    )
    received_data = lax.all_to_all(
        lax.all_to_all(spectrum_rows, "crate", split_axis=0, concat_axis=3, tiled=True),
        "board",
        split_axis=1,
        concat_axis=3,
        tiled=True,
    )
    position_ids = position_grid.transpose(1, 0, 2).reshape(ANTENNA_INPUTS)
    received_data = received_data.reshape(channel_groups, ANTENNA_INPUTS, 2 * BATCH_SPECTRA)
    antenna = jnp.take(wiring, position_ids)
    place_x = jnp.take(positions[0], antenna)
    place_y = jnp.take(positions[1], antenna)
    gains_slot = jnp.take(gains, antenna, axis=2)
    gain_rows = gains.shape[1]
    first_group = (crate_index * board_list + board_index) * channel_groups
    beam_block = 256
    block_count = BEAMS // beam_block
    dir_blocks = directions.reshape(2, block_count, beam_block).transpose(1, 0, 2)

    def group_power(inputs):
        group_id, columns = inputs
        whole_id = first_group + group_id
        channel = whole_id // SPECTRUM_BATCHES
        gain_row = channel - crate_index * gain_rows
        gain_re = lax.dynamic_index_in_dim(gains_slot[0], gain_row, 0, keepdims=False)
        gain_im = lax.dynamic_index_in_dim(gains_slot[1], gain_row, 0, keepdims=False)

        def block_power(dir_block):
            weight_re, weight_im = beam_weights(
                channel, dir_block, place_x, place_y, gain_re, gain_im
            )
            real_side = jnp.dot(weight_re, columns, preferred_element_type=jnp.float32)
            imag_side = jnp.dot(weight_im, columns, preferred_element_type=jnp.float32)
            beam_re = real_side[:, :BATCH_SPECTRA] - imag_side[:, BATCH_SPECTRA:]
            beam_im = real_side[:, BATCH_SPECTRA:] + imag_side[:, :BATCH_SPECTRA]
            beam_power = (
                (beam_re * beam_re + beam_im * beam_im).reshape(beam_block, BINS, AVG).mean(axis=2)
            )
            return beam_power.astype(jnp.bfloat16)

        return lax.map(block_power, dir_blocks).reshape(BEAMS, BINS)

    powers = lax.map(group_power, (jnp.arange(channel_groups, dtype=jnp.int32), received_data))
    beam_local = BEAMS // crate_list
    dm_local = DMS // board_list
    dm_delays = lax.dynamic_slice_in_dim(delays, board_index * dm_local, dm_local, 1)
    regrouped = lax.all_to_all(powers, "crate", split_axis=1, concat_axis=0, tiled=True)
    empty_table = jnp.zeros((SPECTRUM_BATCHES * FREQ_CHANNELS, beam_local, BINS), jnp.bfloat16)
    portion = lax.all_gather(regrouped, "board", axis=0, tiled=True)
    row_count = portion.shape[0]
    row_ids = jnp.arange(row_count, dtype=jnp.int32)
    source_board = row_ids // (crate_list * channel_groups)
    source_crate = row_ids // channel_groups % crate_list
    whole_ids = (
        source_crate * board_list + source_board
    ) * channel_groups + row_ids % channel_groups
    table = empty_table.at[whole_ids].set(portion)
    series = (
        table.reshape(FREQ_CHANNELS, SPECTRUM_BATCHES, beam_local, BINS)
        .transpose(2, 0, 1, 3)
        .reshape(beam_local, FREQ_CHANNELS, TB)
        .astype(jnp.float32)
    )
    result = dedisperse(series, dm_delays)
    return result


def solution(mesh):
    in_specs = (P(("crate", "board"), None), P(), P(), P(), P(None, "crate", None), P())
    out_specs = P("crate", "board", None)
    return jax.shard_map(shards, mesh=mesh, in_specs=in_specs, out_specs=out_specs, check_vma=False)
```

profile of v0, /device:TPU:1, one launch (start us, length us, event | category | flops | bytes accessed | tf_op | source)
XLA Modules:
  0.0 482.1 jit_solution(1558080321978159391)
XLA Ops:
  0.1 1.5 reshape.310
  1.6 2.3 multiply_convert_fusion.5
  7.0 13.7 %all-to-all-start = ((bf16[32,16,1,4,128]{4,1,3,2,0:T(8,128)(2,1)}), bf16[32,16,1,4,128]{4,1,3,2,0:T(8,128)(2,1)S(1)}, u32[]{:S(2)}, u32[]{:S(2)}) async-start(bf16[32,16,1,4,128]{4,1,3,2,0:T(8,128)(2,1)} %copy.49), calls=%async_computation | async-start | bytes 1048576 | tf_op jit(solution)/shard_map/all_to_all | solution.py:109
  21.2 11.8 %gather_fusion = s32[2048]{0:T(1024)S(1)} fusion(s32[2048]{0:T(1024)S(1)} %copy-done.1, s32[2048]{0:T(1024)S(1)} %broadcast_clamp_fusion.2), kind=kCustom, calls=%fused_computation.2 | custom fusion | bytes 24576 | tf_op jit(solution)/shard_map/jit(_take)/gather | solution.py:117
  34.1 11.8 %gather_fusion.3 = f32[2048]{0:T(1024)S(1)} fusion(f32[2048]{0:T(1024)S(1)} %bitcast.105, s32[2048]{0:T(1024)S(1)} %broadcast_clamp_fusion), kind=kCustom, calls=%fused_computation.1.clone | custom fusion | bytes 24576 | tf_op jit(solution)/shard_map/jit(_take)/gather | solution.py:119
  45.9 11.8 %gather_fusion.2 = f32[2048]{0:T(1024)S(1)} fusion(f32[2048]{0:T(1024)S(1)} %bitcast.104, s32[2048]{0:T(1024)S(1)} %broadcast_clamp_fusion), kind=kCustom, calls=%fused_computation.clone | custom fusion | bytes 24576 | tf_op jit(solution)/shard_map/jit(_take)/gather | solution.py:118
  57.7 14.5 %gather_fusion.1 = f32[2048,2,8]{2,1,0:T(2,128)} fusion(f32[2,8,2048]{1,0,2:T(2,128)S(1)} %copy.46, s32[2048]{0:T(1024)S(1)} %broadcast_clamp_fusion.1), kind=kCustom, calls=%fused_computation.3 | custom fusion | bytes 270336 | tf_op jit(solution)/shard_map/jit(_take)/gather | solution.py:120
  72.2 10.0 %select_bitcast_fusion = f32[2,8,2048]{1,0,2:T(2,128)S(1)} fusion(f32[2048,2,8]{2,1,0:T(2,128)} %gather_fusion.1, pred[2048]{0:T(1024)(128)(4,1)S(1)} %get-tuple-element.303), kind=kLoop, calls=%fused_computation.56 | loop fusion | flops 32768 | bytes 264192 | tf_op jit(solution)/shard_map/jit(_take)/select_n | solution.py:120
  83.1 8.6 %all-to-all-start.1 = ((bf16[1,16,1,128,128]{4,3,2,0,1:T(8,128)(2,1)}), bf16[1,16,1,128,128]{4,3,2,0,1:T(8,128)(2,1)}, u32[]{:S(2)}, u32[]{:S(2)}) async-start(bf16[1,16,1,128,128]{4,3,2,0,1:T(8,128)(2,1)} %copy.50), calls=%async_computation.1 | async-start | bytes 1048576 | tf_op jit(solution)/shard_map/all_to_all | solution.py:108
  91.8 1.7 fusion.92
  93.5 57.0 %dynamic-slice_reduce_fusion = (f32[2048]{0:T(1024)S(1)}, f32[2048]{0:T(1024)S(1)}) fusion(f32[1,8,2048]{1,0,2:T(1,128)S(1)} %get-tuple-element.308, s32[]{:T(128)S(6)} %select_n.164, f32[1,8,2048]{1,0,2:T(1,128)S(1)} %get-tuple-element.309), kind=kLoop, calls=%fused_computation.65 | loop fusion | bytes 32772 | tf_op jit(solution)/shard_map/while/body/eval_jaxpr/jit(dynamic_index_in_dim)/dynamic_slice | solution.py:133
  150.6 48.7 %while.33 = (s32[]{:T(128)}, bf16[2,256,16]{1,2,0:T(8,128)(2,1)S(1)}, f32[2048]{0:T(1024)S(1)}, f32[]{:T(128)}, f32[2,2,256]{2,1,0:T(2,128)S(1)}, /*index=5*/f32...) while((s32[]{:T(128)}, ...), condition=%wide.region_2.4_spmd, body=%wide.region_0.3_spmd.sunk | while | flops 277975040 | bytes 1949857 | solution.py:148
  162.4 9.1 %fusion.116 = f32[256,128]{0,1:T(8,128)S(1)} fusion(bf16[2048,128]{1,0:T(8,128)(2,1)} %get-tuple-element.456, f32[2048]{0:T(1024)S(1)} %get-tuple-element.455, f32[2048]{0:T(1024)S(1)} %get-tuple-element.454, f32[256]{0:T(256)S(1)} %bitcast.120, f32[2048]{0:T(1024)S(1)} %get-tuple-element.453, f32[256]{0:T(256)S(1)} %bitcast.118, ...), kind=kOutput, calls=%fused_computation.10.clone.1 | convolution fusion | flops 138936320 | bytes 690180 | tf_op jit(solution)/shard_map/while/body/eval_jaxpr/while/body/eval_jaxpr/dot_general | solution.py:139
  171.5 9.1 %fusion.115 = f32[256,128]{0,1:T(8,128)S(1)} fusion(bf16[2048,128]{1,0:T(8,128)(2,1)} %get-tuple-element.456, f32[2048]{0:T(1024)S(1)} %get-tuple-element.455, f32[2048]{0:T(1024)S(1)} %get-tuple-element.454, f32[256]{0:T(256)S(1)} %bitcast.121, f32[2048]{0:T(1024)S(1)} %get-tuple-element.453, f32[256]{0:T(256)S(1)} %bitcast.119, ...), kind=kOutput, calls=%fused_computation.11.clone.1 | convolution fusion | flops 138936320 | bytes 690180 | tf_op jit(solution)/shard_map/while/body/eval_jaxpr/while/body/eval_jaxpr/dot_general | solution.py:140
  180.8 9.1 %fusion.116 = f32[256,128]{0,1:T(8,128)S(1)} fusion(bf16[2048,128]{1,0:T(8,128)(2,1)} %get-tuple-element.456, f32[2048]{0:T(1024)S(1)} %get-tuple-element.455, f32[2048]{0:T(1024)S(1)} %get-tuple-element.454, f32[256]{0:T(256)S(1)} %bitcast.120, f32[2048]{0:T(1024)S(1)} %get-tuple-element.453, f32[256]{0:T(256)S(1)} %bitcast.118, ...), kind=kOutput, calls=%fused_computation.10.clone.1 | convolution fusion | flops 138936320 | bytes 690180 | tf_op jit(solution)/shard_map/while/body/eval_jaxpr/while/body/eval_jaxpr/dot_general | solution.py:139
  189.9 9.1 %fusion.115 = f32[256,128]{0,1:T(8,128)S(1)} fusion(bf16[2048,128]{1,0:T(8,128)(2,1)} %get-tuple-element.456, f32[2048]{0:T(1024)S(1)} %get-tuple-element.455, f32[2048]{0:T(1024)S(1)} %get-tuple-element.454, f32[256]{0:T(256)S(1)} %bitcast.121, f32[2048]{0:T(1024)S(1)} %get-tuple-element.453, f32[256]{0:T(256)S(1)} %bitcast.119, ...), kind=kOutput, calls=%fused_computation.11.clone.1 | convolution fusion | flops 138936320 | bytes 690180 | tf_op jit(solution)/shard_map/while/body/eval_jaxpr/while/body/eval_jaxpr/dot_general | solution.py:140
  200.0 1.4 reduce.4
  202.2 9.5 %all-to-all-start.2 = ((bf16[32,2,128]{2,1,0:T(2,128)(2,1)}), bf16[32,2,128]{2,1,0:T(2,128)(2,1)S(1)}, u32[]{:S(2)}, u32[]{:S(2)}) async-start(bf16[32,2,128]{2,1,0:T(2,128)(2,1)} %reshape.373), calls=%async_computation.2 | async-start | bytes 32768 | tf_op jit(solution)/shard_map/all_to_all | solution.py:154
  211.8 8.5 %all-to-all-done.2 = bf16[32,2,128]{2,1,0:T(2,128)(2,1)S(1)} async-done(((bf16[32,2,128]{2,1,0:T(2,128)(2,1)}), bf16[32,2,128]{2,1,0:T(2,128)(2,1)S(1)}, u32[]{:S(2)}, u32[]{:S(2)}) %all-to-all-start.2) | async-done | bytes 16416 | tf_op jit(solution)/shard_map/all_to_all | solution.py:154
  220.7 24.8 %all_gather.3 = bf16[512,16,16]{1,0,2:T(8,128)(2,1)S(1)} all-gather(bf16[32,16,16]{1,0,2:T(8,128)(2,1)S(1)} %all_to_all.35), channel_id=1, replica_groups=mesh['crate'=32,'board'=16] {'board'}, dimensions={0}, use_global_device_ids=true | all-gather | bytes 278528 | tf_op jit(solution)/shard_map/all_gather | solution.py:156
  245.5 3.1 copy.54
  248.9 33.1 %scatter_fusion = bf16[512,16,16]{2,1,0:T(8,128)(2,1)S(1)} fusion(bf16[512,16,16]{2,1,0:T(8,128)(2,1)S(1)} %broadcast_in_dim.62, s32[512]{0:T(512)S(1)} %bitcast.123, bf16[512,16,16]{2,1,0:T(8,128)(2,1)} %copy.54), kind=kCustom, calls=%fused_computation.4 | custom fusion | bytes 788480 | tf_op jit(solution)/shard_map/scatter | solution.py:164
  282.0 1.9 copy.55
  284.8 195.4 %while.34 = (s32[]{:T(128)}, f32[32,32,16]{1,0,2:T(8,128)S(1)}, f32[32,32,16]{1,0,2:T(8,128)S(1)}, s32[32]{0:T(128)S(1)}, s32[256,32]{1,0:T(8,128)S(1)}, /*index...) while((s32[]{:T(128)}, f32[32,32,16]{1,0,2:T(8,128)S(1)}, ...), condition=%wide.region_5.7_spmd, body=%wide.region_4.6_spmd.sunk | while | flops 6751234 | bytes 282757 | solution.py:73
  286.8 1.3 convolution_add_fusion.2
  289.5 1.3 convolution_subtract_fusion.3
  292.9 1.3 convolution_add_fusion.2
  295.6 1.3 convolution_subtract_fusion.3
  299.0 1.3 convolution_add_fusion.2
  301.7 1.3 convolution_subtract_fusion.3
  305.1 1.3 convolution_add_fusion.2
  307.8 1.3 convolution_subtract_fusion.3
  (312 shorter events, 193.0 us)
Async XLA Ops:
  0.0 91.7 %copy-start = (s32[256,512]{1,0:T(8,128)S(1)}, s32[256,512]{1,0:T(8,128)}, u32[]{:S(2)}) copy-start(s32[256,512]{1,0:T(8,128)} %param.17) | copy-start | bytes 1572868
  5.6 15.5 %copy-start.4 = (f32[2,2048]{1,0:T(2,128)S(1)}, f32[2,2048]{1,0:T(2,128)}, u32[]{:S(2)}) copy-start(f32[2,2048]{1,0:T(2,128)} %param.14) | copy-start | bytes 49156
  5.6 15.6 %copy-start.1 = (s32[2048]{0:T(1024)S(1)}, s32[2048]{0:T(1024)}, u32[]{:S(2)}) copy-start(s32[2048]{0:T(1024)} %param.13) | copy-start | bytes 24580
  7.0 75.2 %all-to-all-start = ((bf16[32,16,1,4,128]{4,1,3,2,0:T(8,128)(2,1)}), bf16[32,16,1,4,128]{4,1,3,2,0:T(8,128)(2,1)S(1)}, u32[]{:S(2)}, u32[]{:S(2)}) async-start(bf16[32,16,1,4,128]{4,1,3,2,0:T(8,128)(2,1)} %copy.49), calls=%async_computation | async-start | bytes 1048576 | tf_op jit(solution)/shard_map/all_to_all | solution.py:109
  21.2 11.8 %copy-start.2 = (f32[2,8,2048]{2,1,0:T(8,128)S(1)}, f32[2,8,2048]{2,1,0:T(8,128)}, u32[]{:S(2)}) copy-start(f32[2,8,2048]{2,1,0:T(8,128)} %param.16) | copy-start | bytes 393220
  83.1 67.5 %all-to-all-start.1 = ((bf16[1,16,1,128,128]{4,3,2,0,1:T(8,128)(2,1)}), bf16[1,16,1,128,128]{4,3,2,0,1:T(8,128)(2,1)}, u32[]{:S(2)}, u32[]{:S(2)}) async-start(bf16[1,16,1,128,128]{4,3,2,0,1:T(8,128)(2,1)} %copy.50), calls=%async_computation.1 | async-start | bytes 1048576 | tf_op jit(solution)/shard_map/all_to_all | solution.py:108
  93.5 57.1 %copy-start.3 = (f32[2,512]{1,0:T(2,128)S(1)}, f32[2,512]{1,0:T(2,128)}, u32[]{:S(2)}) copy-start(f32[2,512]{1,0:T(2,128)} %param.15) | copy-start | bytes 12292
  202.2 18.0 %all-to-all-start.2 = ((bf16[32,2,128]{2,1,0:T(2,128)(2,1)}), bf16[32,2,128]{2,1,0:T(2,128)(2,1)S(1)}, u32[]{:S(2)}, u32[]{:S(2)}) async-start(bf16[32,2,128]{2,1,0:T(2,128)(2,1)} %reshape.373), calls=%async_computation.2 | async-start | bytes 32768 | tf_op jit(solution)/shard_map/all_to_all | solution.py:154
where the time goes:
time: 490 us; the launch traced here: 482 us
  matrix products  208 us (42%)
  local copies, waits for them, and re-layouts  180 us (37%)
  starting transfers between devices  31.8 us (6%)
  blocking collectives  24.8 us (5%)
  loops' own time  14.4 us (3%)
  other arithmetic  14.1 us (3%)
  waiting for transfers between devices  8.51 us (2%)
    dynamic_slice x1, local copies, waits for them, and re-layouts, group_power(): lax.dynamic_index_in_dim(gains_slot[1], gain_row, 0, keepdims=False)  57 us
    dot_general x32, matrix products, per_freq(): jnp.einsum('cd,cb->db', shift_im, part_re, precision=lax.Precision.HIGHEST)  42.6 us
    dot_general x32, matrix products, per_freq(): jnp.einsum('cd,cb->db', shift_im, part_im, precision=lax.Precision.HIGHEST)  42.6 us
    dot_general x32, matrix products, per_freq(): jnp.einsum('cd,cb->db', shift_re, part_re, precision=lax.Precision.HIGHEST)  42.1 us
    dot_general x32, matrix products, per_freq(): jnp.einsum('cd,cb->db', shift_re, part_im, precision=lax.Precision.HIGHEST)  42 us
    scatter x1, local copies, waits for them, and re-layouts, shards(): table = empty_table.at[whole_ids].set(portion)  33.1 us
    all_gather x1, blocking collectives, shards(): portion = lax.all_gather(regrouped, 'board', axis=0, tiled=True)  24.8 us
    dynamic_slice x64, local copies, waits for them, and re-layouts, dedisperse(): freq_re, freq_im = lax.map(per_freq, (bin_ids, spec_re, spec_im))  20 us
  transfers between devices with their start and end apart: 3, of which 1 were waited for; matrix products, arithmetic and copies ran while one was open for 25% of the time, Pallas kernels for 0%

commit v1 on v0

--- a/solution.py
+++ b/solution.py
@@ -153,7 +153,9 @@
     dm_delays = lax.dynamic_slice_in_dim(delays, board_index * dm_local, dm_local, 1)
     regrouped = lax.all_to_all(powers, "crate", split_axis=1, concat_axis=0, tiled=True)
     empty_table = jnp.zeros((SPECTRUM_BATCHES * FREQ_CHANNELS, beam_local, BINS), jnp.bfloat16)
-    portion = lax.all_gather(regrouped, "board", axis=0, tiled=True)
+    portion = jnp.concatenate(
+        lax.all_to_all(jnp.stack([regrouped] * lax.axis_size("board")), "board", 0, 0), axis=0
+    )
     row_count = portion.shape[0]
     row_ids = jnp.arange(row_count, dtype=jnp.int32)
     source_board = row_ids // (crate_list * channel_groups)

time: 490 us -> 473 us (0.965)
  loops' own time: 14.4 us -> 2.84 us
  blocking collectives: 24.8 us -> 17.9 us
    all_gather x1 -> x0, blocking collectives: 24.8 us -> none  [shards(): portion = lax.all_gather(regrouped, 'board', axis=0, tiled=True)]
    all_to_all x0 -> x1, blocking collectives: none -> 17.9 us  [shards(): lax.all_to_all(powers, 'crate', split_axis=1, concat_axis=0, tiled=True)]
    another operation x1, loops' own time: 12.1 us -> 0.52 us  [group_power(): return lax.map(block_power, dir_blocks).reshape(BEAMS, BINS)]
where the time goes in v1:
time: 473 us; the launch traced here: 464 us
  matrix products  208 us (44%)
  local copies, waits for them, and re-layouts  181 us (38%)
  starting transfers between devices  30.6 us (6%)
  blocking collectives  17.9 us (4%)
  other arithmetic  11.6 us (2%)
  waiting for transfers between devices  11.4 us (2%)
    dynamic_slice x1, local copies, waits for them, and re-layouts, group_power(): lax.dynamic_index_in_dim(gains_slot[1], gain_row, 0, keepdims=False)  57.5 us
    dot_general x32, matrix products, per_freq(): jnp.einsum('cd,cb->db', shift_im, part_re, precision=lax.Precision.HIGHEST)  42.6 us
    dot_general x32, matrix products, per_freq(): jnp.einsum('cd,cb->db', shift_im, part_im, precision=lax.Precision.HIGHEST)  42.6 us
    dot_general x32, matrix products, per_freq(): jnp.einsum('cd,cb->db', shift_re, part_re, precision=lax.Precision.HIGHEST)  42.1 us
    dot_general x32, matrix products, per_freq(): jnp.einsum('cd,cb->db', shift_re, part_im, precision=lax.Precision.HIGHEST)  42 us
    scatter x1, local copies, waits for them, and re-layouts, shards(): table = empty_table.at[whole_ids].set(portion)  33.1 us
    dynamic_slice x64, local copies, waits for them, and re-layouts, dedisperse(): freq_re, freq_im = lax.map(per_freq, (bin_ids, spec_re, spec_im))  20 us
    dot_general x2, matrix products, block_power(): imag_side = jnp.dot(weight_im, columns, preferred_element_type=jnp.float32)  18.2 us
  transfers between devices with their start and end apart: 3, of which 1 were waited for; matrix products, arithmetic and copies ran while one was open for 25% of the time, Pallas kernels for 0%

profile of v1, /device:TPU:1, one launch (start us, length us, event | category | flops | bytes accessed | tf_op | source)
XLA Modules:
  0.0 464.4 jit_solution(4997370888509128410)
XLA Ops:
  0.1 1.5 reshape.315
  1.6 2.3 multiply_convert_fusion.5
  7.0 13.8 %all-to-all-start = ((bf16[32,16,1,4,128]{4,1,3,2,0:T(8,128)(2,1)}), bf16[32,16,1,4,128]{4,1,3,2,0:T(8,128)(2,1)S(1)}, u32[]{:S(2)}, u32[]{:S(2)}) async-start(bf16[32,16,1,4,128]{4,1,3,2,0:T(8,128)(2,1)} %copy.81), calls=%async_computation | async-start | bytes 1048576 | tf_op jit(solution)/shard_map/all_to_all | solution.py:109
  22.3 11.8 %gather_fusion = s32[2048]{0:T(1024)S(1)} fusion(s32[2048]{0:T(1024)S(1)} %copy-done.1, s32[2048]{0:T(1024)S(1)} %broadcast_clamp_fusion.2), kind=kCustom, calls=%fused_computation.2 | custom fusion | bytes 24576 | tf_op jit(solution)/shard_map/jit(_take)/gather | solution.py:117
  34.1 11.8 %gather_fusion.3 = f32[2048]{0:T(1024)S(1)} fusion(f32[2048]{0:T(1024)S(1)} %bitcast.108, s32[2048]{0:T(1024)S(1)} %broadcast_clamp_fusion), kind=kCustom, calls=%fused_computation.1.clone | custom fusion | bytes 24576 | tf_op jit(solution)/shard_map/jit(_take)/gather | solution.py:119
  45.9 11.8 %gather_fusion.2 = f32[2048]{0:T(1024)S(1)} fusion(f32[2048]{0:T(1024)S(1)} %bitcast.107, s32[2048]{0:T(1024)S(1)} %broadcast_clamp_fusion), kind=kCustom, calls=%fused_computation.clone | custom fusion | bytes 24576 | tf_op jit(solution)/shard_map/jit(_take)/gather | solution.py:118
  57.8 14.5 %gather_fusion.1 = f32[2048,2,8]{2,1,0:T(2,128)} fusion(f32[2,8,2048]{1,0,2:T(2,128)S(1)} %copy.78, s32[2048]{0:T(1024)S(1)} %broadcast_clamp_fusion.1), kind=kCustom, calls=%fused_computation.3 | custom fusion | bytes 270336 | tf_op jit(solution)/shard_map/jit(_take)/gather | solution.py:120
  73.2 8.1 %all-to-all-start.1 = ((bf16[1,16,1,128,128]{4,3,2,0,1:T(8,128)(2,1)}), bf16[1,16,1,128,128]{4,3,2,0,1:T(8,128)(2,1)}, u32[]{:S(2)}, u32[]{:S(2)}) async-start(bf16[1,16,1,128,128]{4,3,2,0,1:T(8,128)(2,1)} %copy.82), calls=%async_computation.1 | async-start | bytes 1048576 | tf_op jit(solution)/shard_map/all_to_all | solution.py:108
  81.3 7.4 %select_bitcast_fusion = f32[2,8,2048]{1,0,2:T(2,128)S(1)} fusion(f32[2048,2,8]{2,1,0:T(2,128)S(1)} %copy-done.2, pred[2048]{0:T(1024)(128)(4,1)S(1)} %get-tuple-element.317), kind=kLoop, calls=%fused_computation.56 | loop fusion | flops 32768 | bytes 264192 | tf_op jit(solution)/shard_map/jit(_take)/select_n | solution.py:120
  88.7 1.7 fusion.92
  90.4 57.5 %dynamic-slice_reduce_fusion = (f32[2048]{0:T(1024)S(1)}, f32[2048]{0:T(1024)S(1)}) fusion(f32[1,8,2048]{1,0,2:T(1,128)S(1)} %get-tuple-element.322, s32[]{:T(128)S(6)} %select_n.164, f32[1,8,2048]{1,0,2:T(1,128)S(1)} %get-tuple-element.323), kind=kLoop, calls=%fused_computation.65 | loop fusion | bytes 32772 | tf_op jit(solution)/shard_map/while/body/eval_jaxpr/jit(dynamic_index_in_dim)/dynamic_slice | solution.py:133
  147.9 37.1 %while.33 = (s32[]{:T(128)}, bf16[2,256,16]{1,2,0:T(8,128)(2,1)S(1)}, f32[2048]{0:T(1024)S(1)}, f32[]{:T(128)}, f32[2,2,256]{2,1,0:T(2,128)S(1)}, /*index=5*/f32...) while((s32[]{:T(128)}, ...), condition=%wide.region_2.4_spmd, body=%wide.region_0.3_spmd.sunk | while | flops 277975040 | bytes 1949857 | solution.py:148
  148.1 9.1 %fusion.116 = f32[256,128]{0,1:T(8,128)S(1)} fusion(bf16[2048,128]{1,0:T(8,128)(2,1)} %get-tuple-element.470, f32[2048]{0:T(1024)S(1)} %get-tuple-element.469, f32[2048]{0:T(1024)S(1)} %get-tuple-element.468, f32[256]{0:T(256)S(1)} %bitcast.126, f32[2048]{0:T(1024)S(1)} %get-tuple-element.467, f32[256]{0:T(256)S(1)} %bitcast.124, ...), kind=kOutput, calls=%fused_computation.10.clone.1 | convolution fusion | flops 138936320 | bytes 690180 | tf_op jit(solution)/shard_map/while/body/eval_jaxpr/while/body/eval_jaxpr/dot_general | solution.py:139
  157.3 9.1 %fusion.115 = f32[256,128]{0,1:T(8,128)S(1)} fusion(bf16[2048,128]{1,0:T(8,128)(2,1)} %get-tuple-element.470, f32[2048]{0:T(1024)S(1)} %get-tuple-element.469, f32[2048]{0:T(1024)S(1)} %get-tuple-element.468, f32[256]{0:T(256)S(1)} %bitcast.127, f32[2048]{0:T(1024)S(1)} %get-tuple-element.467, f32[256]{0:T(256)S(1)} %bitcast.125, ...), kind=kOutput, calls=%fused_computation.11.clone.1 | convolution fusion | flops 138936320 | bytes 690180 | tf_op jit(solution)/shard_map/while/body/eval_jaxpr/while/body/eval_jaxpr/dot_general | solution.py:140
  166.5 9.1 %fusion.116 = f32[256,128]{0,1:T(8,128)S(1)} fusion(bf16[2048,128]{1,0:T(8,128)(2,1)} %get-tuple-element.470, f32[2048]{0:T(1024)S(1)} %get-tuple-element.469, f32[2048]{0:T(1024)S(1)} %get-tuple-element.468, f32[256]{0:T(256)S(1)} %bitcast.126, f32[2048]{0:T(1024)S(1)} %get-tuple-element.467, f32[256]{0:T(256)S(1)} %bitcast.124, ...), kind=kOutput, calls=%fused_computation.10.clone.1 | convolution fusion | flops 138936320 | bytes 690180 | tf_op jit(solution)/shard_map/while/body/eval_jaxpr/while/body/eval_jaxpr/dot_general | solution.py:139
  175.6 9.1 %fusion.115 = f32[256,128]{0,1:T(8,128)S(1)} fusion(bf16[2048,128]{1,0:T(8,128)(2,1)} %get-tuple-element.470, f32[2048]{0:T(1024)S(1)} %get-tuple-element.469, f32[2048]{0:T(1024)S(1)} %get-tuple-element.468, f32[256]{0:T(256)S(1)} %bitcast.127, f32[2048]{0:T(1024)S(1)} %get-tuple-element.467, f32[256]{0:T(256)S(1)} %bitcast.125, ...), kind=kOutput, calls=%fused_computation.11.clone.1 | convolution fusion | flops 138936320 | bytes 690180 | tf_op jit(solution)/shard_map/while/body/eval_jaxpr/while/body/eval_jaxpr/dot_general | solution.py:140
  185.8 1.4 reduce.4
  187.4 17.9 %all_to_all.41 = bf16[32,2,128]{2,1,0:T(2,128)(2,1)S(1)} all-to-all(bf16[32,2,128]{2,1,0:T(2,128)(2,1)S(1)} %reshape.380), channel_id=1, replica_groups=mesh['crate'=32,'board'=16] {'crate'}, dimensions={0} | all-to-all | bytes 32768 | tf_op jit(solution)/shard_map/all_to_all | solution.py:154
  205.9 1.7 reshape.382
  207.6 8.7 %all-to-all-start.3 = ((bf16[16,2,4096]{2,1,0:T(2,128)(2,1)}), bf16[16,2,4096]{2,1,0:T(2,128)(2,1)S(1)}, u32[]{:S(2)}, u32[]{:S(2)}) async-start(bf16[16,2,4096]{2,1,0:T(2,128)(2,1)} %reshape.382), calls=%async_computation.3 | async-start | bytes 524288 | tf_op jit(solution)/shard_map/all_to_all | solution.py:157
  216.4 11.4 %all-to-all-done.3 = bf16[16,2,4096]{2,1,0:T(2,128)(2,1)S(1)} async-done(((bf16[16,2,4096]{2,1,0:T(2,128)(2,1)}), bf16[16,2,4096]{2,1,0:T(2,128)(2,1)S(1)}, u32[]{:S(2)}, u32[]{:S(2)}) %all-to-all-start.3) | async-done | bytes 262176 | tf_op jit(solution)/shard_map/all_to_all | solution.py:157
  228.4 2.6 copy.97
  231.2 33.1 %scatter_fusion = bf16[512,16,16]{2,1,0:T(8,128)(2,1)S(1)} fusion(bf16[512,16,16]{2,1,0:T(8,128)(2,1)S(1)} %broadcast_in_dim.62, s32[512]{0:T(512)S(1)} %bitcast.129, bf16[512,16,16]{2,1,0:T(8,128)(2,1)} %bitcast.110), kind=kCustom, calls=%fused_computation.4 | custom fusion | bytes 788480 | tf_op jit(solution)/shard_map/scatter | solution.py:166
  264.3 1.9 copy.89
  267.1 195.4 %while.34 = (s32[]{:T(128)}, f32[32,32,16]{1,0,2:T(8,128)S(1)}, f32[32,32,16]{1,0,2:T(8,128)S(1)}, s32[32]{0:T(128)S(1)}, s32[256,32]{1,0:T(8,128)S(1)}, /*index...) while((s32[]{:T(128)}, f32[32,32,16]{1,0,2:T(8,128)S(1)}, ...), condition=%wide.region_5.7_spmd, body=%wide.region_4.6_spmd.sunk | while | flops 6751234 | bytes 282757 | solution.py:73
  269.1 1.3 convolution_add_fusion.2
  271.8 1.3 convolution_subtract_fusion.3
  275.2 1.3 convolution_add_fusion.2
  277.9 1.3 convolution_subtract_fusion.3
  281.3 1.3 convolution_add_fusion.2
  284.0 1.3 convolution_subtract_fusion.3
  287.4 1.3 convolution_add_fusion.2
  (317 shorter events, 194.3 us)
Async XLA Ops:
  0.0 216.3 %copy-start = (s32[256,512]{1,0:T(8,128)S(1)}, s32[256,512]{1,0:T(8,128)}, u32[]{:S(2)}) copy-start(s32[256,512]{1,0:T(8,128)} %param.17) | copy-start | bytes 1572868
  5.6 15.7 %copy-start.5 = (f32[2,2048]{1,0:T(2,128)S(1)}, f32[2,2048]{1,0:T(2,128)}, u32[]{:S(2)}) copy-start(f32[2,2048]{1,0:T(2,128)} %param.14) | copy-start | bytes 49156
  5.6 15.7 %copy-start.3 = (f32[2,8,2048]{2,1,0:T(8,128)S(1)}, f32[2,8,2048]{2,1,0:T(8,128)}, u32[]{:S(2)}) copy-start(f32[2,8,2048]{2,1,0:T(8,128)} %param.16) | copy-start | bytes 393220
  7.0 15.3 %copy-start.1 = (s32[2048]{0:T(1024)S(1)}, s32[2048]{0:T(1024)}, u32[]{:S(2)}) copy-start(s32[2048]{0:T(1024)} %param.13) | copy-start | bytes 24580
  7.0 65.3 %all-to-all-start = ((bf16[32,16,1,4,128]{4,1,3,2,0:T(8,128)(2,1)}), bf16[32,16,1,4,128]{4,1,3,2,0:T(8,128)(2,1)S(1)}, u32[]{:S(2)}, u32[]{:S(2)}) async-start(bf16[32,16,1,4,128]{4,1,3,2,0:T(8,128)(2,1)} %copy.81), calls=%async_computation | async-start | bytes 1048576 | tf_op jit(solution)/shard_map/all_to_all | solution.py:109
  72.2 9.0 %copy-start.2 = (f32[2048,2,8]{2,1,0:T(2,128)S(1)}, f32[2048,2,8]{2,1,0:T(2,128)}, u32[]{:S(2)}) copy-start(f32[2048,2,8]{2,1,0:T(2,128)} %gather_fusion.1) | copy-start | bytes 393220
  73.2 74.7 %all-to-all-start.1 = ((bf16[1,16,1,128,128]{4,3,2,0,1:T(8,128)(2,1)}), bf16[1,16,1,128,128]{4,3,2,0,1:T(8,128)(2,1)}, u32[]{:S(2)}, u32[]{:S(2)}) async-start(bf16[1,16,1,128,128]{4,3,2,0,1:T(8,128)(2,1)} %copy.82), calls=%async_computation.1 | async-start | bytes 1048576 | tf_op jit(solution)/shard_map/all_to_all | solution.py:108
  90.4 57.5 %copy-start.4 = (f32[2,512]{1,0:T(2,128)S(1)}, f32[2,512]{1,0:T(2,128)}, u32[]{:S(2)}) copy-start(f32[2,512]{1,0:T(2,128)} %param.15) | copy-start | bytes 12292
  207.6 20.2 %all-to-all-start.3 = ((bf16[16,2,4096]{2,1,0:T(2,128)(2,1)}), bf16[16,2,4096]{2,1,0:T(2,128)(2,1)S(1)}, u32[]{:S(2)}, u32[]{:S(2)}) async-start(bf16[16,2,4096]{2,1,0:T(2,128)(2,1)} %reshape.382), calls=%async_computation.3 | async-start | bytes 524288 | tf_op jit(solution)/shard_map/all_to_all | solution.py:157
